TPU v7x, 256 devices: a whole 4x4x8 slice. The times are simulated.
256 devices in a mesh: rep: 64 (over z, y, core), shard: 4 (over x).
Axes of the slice: x: 4, y: 4, z: 8, core: 2. Of those that a mesh axis runs over, the one named last changes fastest.
Arguments:
- q_grad: float32 [64, 1152, 1152], P('rep', None, 'shard'), may hold values from -16 to 16
- o_grad: float32 [64, 1152, 1152], P('rep', None, 'shard'), may hold values from -16 to 16
- q_error: float32 [64, 1152, 1152], P('rep', None, 'shard'), may hold values from -4 to 4
- o_error: float32 [64, 1152, 1152], P('rep', None, 'shard'), may hold values from -4 to 4
- q_basis: float32 [1152, 32], P('shard'), may hold values from -6 to 6
- o_basis: float32 [1152, 32], P('shard'), may hold values from -6 to 6
- q_moment: float32 [1152, 1152], P('rep', 'shard'), may hold values from -6 to 6
- o_moment: float32 [1152, 1152], P('rep', 'shard'), may hold values from -6 to 6
- q_weight: float32 [1152, 1152], P('rep', 'shard'), may hold values from -0.1875 to 0.1875
- o_weight: float32 [1152, 1152], P('rep', 'shard'), may hold values from -0.1875 to 0.1875
- norm_grads: float32 [64, 4, 2304], P('rep', 'shard'), may hold values from -6 to 6
- norm_moment: float32 [2304], P(('rep', 'shard')), may hold values from -6 to 6
- norm_weight: float32 [2304], P(('rep', 'shard')), may hold values from 0.5 to 1.5
Outputs:
- q_weight_new: float32 [1152, 1152], P(None, 'shard')
- o_weight_new: float32 [1152, 1152], P(None, 'shard')
- q_moment_new: float32 [1152, 1152], P('rep', 'shard')
- o_moment_new: float32 [1152, 1152], P('rep', 'shard')
- q_error_new: float32 [64, 1152, 1152], P('rep', None, 'shard')
- o_error_new: float32 [64, 1152, 1152], P('rep', None, 'shard')
- norm_weight_new: float32 [2304], replicated
- norm_moment_new: float32 [2304], P(('rep', 'shard'))
All inputs are finite; a program needn't handle non-finite values.
Results may differ from a plain program's by a relative error of at most 0.0003.
Values sent between devices are 32-bit elements; how exact they have to be, the bound alone decides.
A program may use at most 64 MiB of HBM per device.

v0:
```python
import jax
import jax.numpy as jnp
from jax import lax
from jax.sharding import PartitionSpec as P

ROUNDS = 2
highest = lax.Precision.HIGHEST
decay_rate = 0.9
step_size = 0.1


def unwhiten(lower, factor):
    return jax.scipy.linalg.solve_triangular(lower, factor.T, lower=True).T


def product(left, right):
    return jnp.dot(left, right, precision=highest)


def per_device(
    q_grad,
    o_grad,
    q_error,
    o_error,
    q_basis,
    o_basis,
    q_moment,
    o_moment,
    q_weight,
    o_weight,
    norm_grads,
    norm_moment,
    norm_weight,
):
    corr_q = q_grad[0] + q_error[0]
    corr_o = o_grad[0] + o_error[0]
    basis_q = q_basis
    basis_o = o_basis
    normal_q = None
    normal_o = None
    for sweep in range(ROUNDS):
        part_q = product(corr_q, basis_q)
        part_o = product(corr_o, basis_o)
        left_q, left_o = lax.psum((part_q, part_o), ("rep", "shard"))
        gram_q = product(left_q.T, left_q)
        gram_o = product(left_o.T, left_o)
        lower_q = jnp.linalg.cholesky(gram_q)
        lower_o = jnp.linalg.cholesky(gram_o)
        normal_q = unwhiten(lower_q, left_q)
        normal_o = unwhiten(lower_o, left_o)
        reduce_q = product(corr_q.T, normal_q)
        reduce_o = product(corr_o.T, normal_o)
        summed_q, summed_o = lax.psum((reduce_q, reduce_o), "rep")
        basis_q = summed_q
        basis_o = summed_o
    decoded_q = product(normal_q, basis_q.T)
    decoded_o = product(normal_o, basis_o.T)
    q_error_new = (corr_q - decoded_q)[None]
    o_error_new = (corr_o - decoded_o)[None]
    row_count = q_moment.shape[0]
    start = lax.axis_index("rep") * row_count
    slice_q = lax.dynamic_slice_in_dim(decoded_q, start, row_count, 0)
    slice_o = lax.dynamic_slice_in_dim(decoded_o, start, row_count, 0)
    q_moment_new = decay_rate * q_moment + slice_q
    o_moment_new = decay_rate * o_moment + slice_o
    weight_q = q_weight - step_size * q_moment_new
    weight_o = o_weight - step_size * o_moment_new
    q_weight_new, o_weight_new = (
        lax.all_gather(weight_q, "rep", axis=0, tiled=True),
        lax.all_gather(weight_o, "rep", axis=0, tiled=True),
    )
    flat_grads = norm_grads.reshape(-1)
    norm_sum = lax.psum_scatter(flat_grads, ("rep", "shard"), scatter_dimension=0, tiled=True)
    norm_moment_new = decay_rate * norm_moment + norm_sum
    gain_share = norm_weight - step_size * norm_moment_new
    norm_weight_new = lax.all_gather(gain_share, ("rep", "shard"), axis=0, tiled=True)
    return (
        q_weight_new,
        o_weight_new,
        q_moment_new,
        o_moment_new,
        q_error_new,
        o_error_new,
        norm_weight_new,
        norm_moment_new,
    )


def solution(mesh):
    return jax.shard_map(
        per_device,
        mesh=mesh,
        in_specs=(
            P("rep", None, "shard"),
            P("rep", None, "shard"),
            P("rep", None, "shard"),
            P("rep", None, "shard"),
            P("shard", None),
            P("shard", None),
            P("rep", "shard"),
            P("rep", "shard"),
            P("rep", "shard"),
            P("rep", "shard"),
            P("rep", "shard", None),
            P(("rep", "shard")),
            P(("rep", "shard")),
        ),
        out_specs=(
            P(None, "shard"),
            P(None, "shard"),
            P("rep", "shard"),
            P("rep", "shard"),
            P("rep", None, "shard"),
            P("rep", None, "shard"),
            P(),
            P(("rep", "shard")),
        ),
        check_vma=False,
    )
```

profile of v0, /device:TPU:1, one launch (start us, length us, event | category | flops | bytes accessed | tf_op | source)
XLA Modules:
  0.0 1079.3 jit_solution(495348832060264353)
XLA Ops:
  7.2 2.0 add.52
  9.2 1.6 fusion.15
  11.6 1.6 fusion.6
  13.3 252.6 %all-reduce.13.cloned.1.call-done = (f32[1152,32]{0,1:T(8,128)}, f32[1152,32]{0,1:T(8,128)}) async-done(((f32[1152,32]{0,1:T(8,128)}, f32[1152,32]{0,1:T(8,128)}), (f32[1152,32]{0,1:T(8,128)}, f32[1152,32]{0,1:T(8,128)})) %all-reduce.13.cloned.1.call-update) | async-done | bytes 294928 | tf_op jit(solution)/shard_map/psum | solution.py:44
  265.9 1.3 fusion.40
  268.5 2.9 cholesky.96
  272.8 2.4 custom-call.10
  276.5 1.8 fusion.4
  278.4 2.9 cholesky.74
  282.7 2.4 custom-call.8
  285.5 1.8 fusion.13
  287.4 169.6 %all-reduce.17.cloned.1.call-done = (f32[288,32]{0,1:T(8,128)}, f32[288,32]{0,1:T(8,128)}) async-done(((f32[288,32]{0,1:T(8,128)}, f32[288,32]{0,1:T(8,128)}), (f32[288,32]{0,1:T(8,128)}, f32[288,32]{0,1:T(8,128)})) %all-reduce.17.cloned.1.call-update) | async-done | bytes 73744 | tf_op jit(solution)/shard_map/psum | solution.py:53
  457.0 2.4 fusion.11
  459.4 1.6 fusion.2
  461.3 247.8 %all-reduce.11.cloned.1.call-done = (f32[1152,32]{0,1:T(8,128)}, f32[1152,32]{0,1:T(8,128)}) async-done(((f32[1152,32]{0,1:T(8,128)}, f32[1152,32]{0,1:T(8,128)}), (f32[1152,32]{0,1:T(8,128)}, f32[1152,32]{0,1:T(8,128)})) %all-reduce.11.cloned.1.call-update) | async-done | bytes 294928 | tf_op jit(solution)/shard_map/psum | solution.py:44
  711.6 2.9 cholesky.107
  715.9 2.4 custom-call.11
  719.7 2.9 cholesky.85
  723.9 2.4 custom-call.9
  727.7 1.8 fusion.9
  729.5 1.8 fusion
  732.6 168.4 %all-reduce.15.cloned.1.call-done = (f32[288,32]{0,1:T(8,128)}, f32[288,32]{0,1:T(8,128)}) async-done(((f32[288,32]{0,1:T(8,128)}, f32[288,32]{0,1:T(8,128)}), (f32[288,32]{0,1:T(8,128)}, f32[288,32]{0,1:T(8,128)})) %all-reduce.15.cloned.1.call-update) | async-done | bytes 73744 | tf_op jit(solution)/shard_map/psum | solution.py:53
  901.0 2.1 fusion.42
  906.3 1.6 copy.54
  908.1 1.6 copy.49
  909.8 77.3 %all-reduce.1 = f32[2304]{0:T(1024)S(1)} all-reduce(f32[2304]{0:T(1024)S(1)} %reduce.4), channel_id=2, replica_groups=mesh['rep'=64,'shard'=4] {'rep','shard'}, use_global_device_ids=true, to_apply=%region_10.13.clone | all-reduce | flops 2304 | bytes 18432
  987.8 73.1 %all-reduce = f32[2304]{0:T(1024)} all-reduce(f32[2304]{0:T(1024)S(1)} %get-tuple-element.42), channel_id=1, replica_groups=mesh['rep'=64,'shard'=4] {'rep','shard'}, use_global_device_ids=true, to_apply=%add | all-reduce | flops 2304 | bytes 18432
  1062.3 3.5 fusion.8
  1065.8 1.7 reshape.35
  1067.6 1.6 copy.56
  1069.1 1.7 reshape.33
  1070.9 1.6 copy.55
  (87 shorter events, 21.3 us)
Async XLA Ops:
  7.2 2.0 copy-start
  7.2 258.7 %all-reduce.13.cloned.1.call-start = ((), (), s32[]{:S(2)}) async-start(), calls=%async_computation.3 | async-start | bytes 589824 | tf_op jit(solution)/shard_map/psum | solution.py:44
  7.2 3.6 copy-start.5
  9.2 1.6 copy-start.4
  10.8 0.8 copy-start.7
  13.2 443.8 %all-reduce.17.cloned.1.call-start = ((), (), s32[]{:S(2)}) async-start(), calls=%async_computation.5 | async-start | bytes 196608 | tf_op jit(solution)/shard_map/psum | solution.py:53
  265.9 19.2 %copy-start.3 = (f32[1152,32]{0,1:T(8,128)S(1)}, f32[1152,32]{0,1:T(8,128)}, u32[]{:S(2)}) copy-start(f32[1152,32]{0,1:T(8,128)} %get-tuple-element.36) | copy-start | bytes 442372
  287.4 421.7 %all-reduce.11.cloned.1.call-start = ((), (), s32[]{:S(2)}) async-start(), calls=%async_computation.2 | async-start | bytes 589824 | tf_op jit(solution)/shard_map/psum | solution.py:44
  457.0 2.4 copy-start.9
  461.0 440.0 %all-reduce.15.cloned.1.call-start = ((), (), s32[]{:S(2)}) async-start(), calls=%async_computation.4 | async-start | bytes 196608 | tf_op jit(solution)/shard_map/psum | solution.py:53
  727.6 3.8 copy-start.10
  727.7 3.9 copy-start.11
  729.5 2.2 copy-start.12
  729.5 2.3 copy-start.13
  731.4 334.4 %all-gather.7.cloned.1.call-start = ((), (), s32[]{:S(2)}) async-start(), calls=%async_computation.1 | async-start | bytes 2396160 | tf_op jit(solution)/shard_map/all_gather | solution.py:70
  901.0 2.1 copy-start.8
  901.0 4.4 copy-start.6
  903.1 3.2 copy-start.1
  904.4 1.1 copy-start.2
  905.5 4.3 copy-start.14
  905.5 81.7 %copy-start.15 = (f32[9]{0:T(128)S(1)}, f32[9]{0:T(128)}, u32[]{:S(2)}) copy-start(f32[9]{0:T(128)} %param.28) | copy-start | bytes 112
  905.5 81.7 %copy-start.16 = (f32[9]{0:T(128)S(1)}, f32[9]{0:T(128)}, u32[]{:S(2)}) copy-start(f32[9]{0:T(128)} %param.27) | copy-start | bytes 112
  908.0 161.1 %all-gather.5.cloned.1.call-start = ((), (), s32[]{:S(2)}) async-start(), calls=%async_computation | async-start | bytes 2396160 | tf_op jit(solution)/shard_map/all_gather | solution.py:69
Sparse Core Ops, SparseCore 0:
  14.2 251.6 all-reduce.12
  287.5 169.5 all-reduce.16
  463.2 245.7 all-reduce.10
  731.5 169.4 all-reduce.14
  908.1 75.9 all-gather.6
  986.6 75.1 all-gather.4
where the time goes:
time: 1080 us
  waiting for transfers between devices  839 us (78%)
  blocking collectives  150 us (14%)
  other arithmetic  33.9 us (3%)
  matrix products  27.1 us (3%)
  local copies, waits for them, and re-layouts  14.5 us (1%)
  between operations  14.4 us (1%)
    psum x2, waiting for transfers between devices, per_device(): left_q, left_o = lax.psum((part_q, part_o), ('rep', 'shard'))  500 us
    psum x2, waiting for transfers between devices, per_device(): summed_q, summed_o = lax.psum((reduce_q, reduce_o), 'rep')  338 us
    unnamed x2, blocking collectives  150 us
    dot_general x14, matrix products, product(): return jnp.dot(left, right, precision=highest)  22.9 us
  transfers between devices with their start and end apart: 6, of which 4 were waited for; matrix products, arithmetic and copies ran while one was open for 1% of the time, Pallas kernels for 0%

commit v1 on v0

--- a/solution.py
+++ b/solution.py
@@ -41,7 +41,7 @@
     for sweep in range(ROUNDS):
         part_q = product(corr_q, basis_q)
         part_o = product(corr_o, basis_o)
-        left_q, left_o = lax.psum((part_q, part_o), ("rep", "shard"))
+        left_q, left_o = lax.psum(lax.psum((part_q, part_o), "shard"), "rep")
         gram_q = product(left_q.T, left_q)
         gram_o = product(left_o.T, left_o)
         lower_q = jnp.linalg.cholesky(gram_q)

time: 1080 us -> 1040 us (0.963)
  waiting for transfers between devices: 839 us -> 802 us
    psum x2 -> x4, waiting for transfers between devices: 500 us -> 461 us  [per_device(): left_q, left_o = lax.psum(lax.psum((part_q, part_o), 'shard'), 'rep')]
  transfers between devices with their start and end apart: 6 -> 8, of which waited for: 4 -> 6; matrix products, arithmetic and copies ran while one was open for 1% -> 1% of each run, Pallas kernels for 0% -> 0%
where the time goes in v1:
time: 1040 us
  waiting for transfers between devices  802 us (77%)
  blocking collectives  151 us (15%)
  other arithmetic  33.9 us (3%)
  matrix products  27.1 us (3%)
  local copies, waits for them, and re-layouts  14.5 us (1%)
  between operations  14.5 us (1%)
    psum x4, waiting for transfers between devices, per_device(): left_q, left_o = lax.psum(lax.psum((part_q, part_o), 'shard'), 'rep')  461 us
    psum x2, waiting for transfers between devices, per_device(): summed_q, summed_o = lax.psum((reduce_q, reduce_o), 'rep')  341 us
    unnamed x2, blocking collectives  151 us
    dot_general x14, matrix products, product(): return jnp.dot(left, right, precision=highest)  22.9 us
  transfers between devices with their start and end apart: 8, of which 6 were waited for; matrix products, arithmetic and copies ran while one was open for 1% of the time, Pallas kernels for 0%

profile of v1, /device:TPU:1, one launch (start us, length us, event | category | flops | bytes accessed | tf_op | source)
XLA Modules:
  0.0 1042.8 jit_solution(5659803415435870185)
XLA Ops:
  7.2 2.0 add.60
  9.2 1.6 fusion.15
  11.6 1.6 fusion.6
  13.3 48.9 %all-reduce.25.cloned.1.call-done = (f32[1152,32]{0,1:T(8,128)}, f32[1152,32]{0,1:T(8,128)}) async-done(((f32[1152,32]{0,1:T(8,128)}, f32[1152,32]{0,1:T(8,128)}), (f32[1152,32]{0,1:T(8,128)}, f32[1152,32]{0,1:T(8,128)})) %all-reduce.25.cloned.1.call-update) | async-done | bytes 294928 | tf_op jit(solution)/shard_map/psum | solution.py:44
  62.2 184.8 %all-reduce.21.cloned.1.call-done = (f32[1152,32]{0,1:T(8,128)}, f32[1152,32]{0,1:T(8,128)}) async-done(((f32[1152,32]{0,1:T(8,128)}, f32[1152,32]{0,1:T(8,128)}), (f32[1152,32]{0,1:T(8,128)}, f32[1152,32]{0,1:T(8,128)})) %all-reduce.21.cloned.1.call-update) | async-done | bytes 294928 | tf_op jit(solution)/shard_map/psum | solution.py:44
  249.7 2.9 cholesky.96
  253.9 2.4 custom-call.10
  257.6 1.8 fusion.4
  259.5 2.9 cholesky.74
  263.8 2.4 custom-call.8
  266.6 1.8 fusion.13
  268.5 170.8 %all-reduce.17.cloned.1.call-done = (f32[288,32]{0,1:T(8,128)}, f32[288,32]{0,1:T(8,128)}) async-done(((f32[288,32]{0,1:T(8,128)}, f32[288,32]{0,1:T(8,128)}), (f32[288,32]{0,1:T(8,128)}, f32[288,32]{0,1:T(8,128)})) %all-reduce.17.cloned.1.call-update) | async-done | bytes 73744 | tf_op jit(solution)/shard_map/psum | solution.py:53
  439.4 2.4 fusion.11
  441.8 1.6 fusion.2
  443.4 43.0 %all-reduce.23.cloned.1.call-done = (f32[1152,32]{0,1:T(8,128)}, f32[1152,32]{0,1:T(8,128)}) async-done(((f32[1152,32]{0,1:T(8,128)}, f32[1152,32]{0,1:T(8,128)}), (f32[1152,32]{0,1:T(8,128)}, f32[1152,32]{0,1:T(8,128)})) %all-reduce.23.cloned.1.call-update) | async-done | bytes 294928 | tf_op jit(solution)/shard_map/psum | solution.py:44
  486.7 184.4 %all-reduce.19.cloned.1.call-done = (f32[1152,32]{0,1:T(8,128)}, f32[1152,32]{0,1:T(8,128)}) async-done(((f32[1152,32]{0,1:T(8,128)}, f32[1152,32]{0,1:T(8,128)}), (f32[1152,32]{0,1:T(8,128)}, f32[1152,32]{0,1:T(8,128)})) %all-reduce.19.cloned.1.call-update) | async-done | bytes 294928 | tf_op jit(solution)/shard_map/psum | solution.py:44
  673.7 2.9 cholesky.107
  677.9 2.4 custom-call.11
  681.7 2.9 cholesky.85
  686.0 2.4 custom-call.9
  689.7 1.8 fusion.9
  691.6 1.8 fusion
  694.6 169.8 %all-reduce.15.cloned.1.call-done = (f32[288,32]{0,1:T(8,128)}, f32[288,32]{0,1:T(8,128)}) async-done(((f32[288,32]{0,1:T(8,128)}, f32[288,32]{0,1:T(8,128)}), (f32[288,32]{0,1:T(8,128)}, f32[288,32]{0,1:T(8,128)})) %all-reduce.15.cloned.1.call-update) | async-done | bytes 73744 | tf_op jit(solution)/shard_map/psum | solution.py:53
  864.5 2.1 fusion.42
  869.8 1.6 copy.54
  871.5 1.6 copy.49
  873.2 77.3 %all-reduce.1 = f32[2304]{0:T(1024)S(1)} all-reduce(f32[2304]{0:T(1024)S(1)} %reduce.4), channel_id=2, replica_groups=mesh['rep'=64,'shard'=4] {'rep','shard'}, use_global_device_ids=true, to_apply=%region_14.17.clone | all-reduce | flops 2304 | bytes 18432
  951.2 73.2 %all-reduce = f32[2304]{0:T(1024)} all-reduce(f32[2304]{0:T(1024)S(1)} %get-tuple-element.46), channel_id=1, replica_groups=mesh['rep'=64,'shard'=4] {'rep','shard'}, use_global_device_ids=true, to_apply=%add | all-reduce | flops 2304 | bytes 18432
  1025.8 3.5 fusion.8
  1029.3 1.7 reshape.35
  1031.1 1.6 copy.56
  1032.7 1.7 reshape.33
  (93 shorter events, 24.3 us)
Async XLA Ops:
  7.2 2.0 copy-start
  7.2 55.0 %all-reduce.25.cloned.1.call-start = ((), (), s32[]{:S(2)}) async-start(), calls=%async_computation.7 | async-start | bytes 589824 | tf_op jit(solution)/shard_map/psum | solution.py:44
  7.2 3.6 copy-start.5
  9.2 1.6 copy-start.4
  10.8 0.8 copy-start.7
  13.2 233.8 %all-reduce.21.cloned.1.call-start = ((), (), s32[]{:S(2)}) async-start(), calls=%async_computation.5 | async-start | bytes 589824 | tf_op jit(solution)/shard_map/psum | solution.py:44
  62.2 377.2 %all-reduce.17.cloned.1.call-start = ((), (), s32[]{:S(2)}) async-start(), calls=%async_computation.3 | async-start | bytes 196608 | tf_op jit(solution)/shard_map/psum | solution.py:53
  247.0 19.2 %copy-start.3 = (f32[1152,32]{0,1:T(8,128)S(1)}, f32[1152,32]{0,1:T(8,128)}, u32[]{:S(2)}) copy-start(f32[1152,32]{0,1:T(8,128)} %get-tuple-element.40) | copy-start | bytes 442372
  268.5 218.0 %all-reduce.23.cloned.1.call-start = ((), (), s32[]{:S(2)}) async-start(), calls=%async_computation.6 | async-start | bytes 589824 | tf_op jit(solution)/shard_map/psum | solution.py:44
  439.4 2.4 copy-start.9
  443.4 227.7 %all-reduce.19.cloned.1.call-start = ((), (), s32[]{:S(2)}) async-start(), calls=%async_computation.4 | async-start | bytes 589824 | tf_op jit(solution)/shard_map/psum | solution.py:44
  486.4 378.0 %all-reduce.15.cloned.1.call-start = ((), (), s32[]{:S(2)}) async-start(), calls=%async_computation.2 | async-start | bytes 196608 | tf_op jit(solution)/shard_map/psum | solution.py:53
  689.7 3.8 copy-start.10
  689.7 3.9 copy-start.11
  691.6 2.2 copy-start.12
  691.6 2.3 copy-start.13
  693.4 335.9 %all-gather.7.cloned.1.call-start = ((), (), s32[]{:S(2)}) async-start(), calls=%async_computation.1 | async-start | bytes 2396160 | tf_op jit(solution)/shard_map/all_gather | solution.py:70
  864.5 2.1 copy-start.8
  864.5 4.4 copy-start.6
  866.5 3.2 copy-start.1
  867.8 1.1 copy-start.2
  868.9 4.3 copy-start.14
  868.9 81.7 %copy-start.15 = (f32[9]{0:T(128)S(1)}, f32[9]{0:T(128)}, u32[]{:S(2)}) copy-start(f32[9]{0:T(128)} %param.28) | copy-start | bytes 112
  868.9 81.7 %copy-start.16 = (f32[9]{0:T(128)S(1)}, f32[9]{0:T(128)}, u32[]{:S(2)}) copy-start(f32[9]{0:T(128)} %param.27) | copy-start | bytes 112
  871.4 161.2 %all-gather.5.cloned.1.call-start = ((), (), s32[]{:S(2)}) async-start(), calls=%async_computation | async-start | bytes 2396160 | tf_op jit(solution)/shard_map/all_gather | solution.py:69
Sparse Core Ops, SparseCore 0:
  13.4 48.7 all-reduce.24
  65.7 181.2 all-reduce.20
  268.6 170.7 all-reduce.16
  443.5 42.8 all-reduce.22
  489.8 181.2 all-reduce.18
  693.6 170.8 all-reduce.14
  871.5 75.9 all-gather.6
  950.2 75.0 all-gather.4
